TPU v7x, 32 devices: a whole 2x2x4 slice. The times are simulated.
32 devices in a mesh: row: 8 (over y, x, core), col: 4 (over z).
Axes of the slice: x: 2, y: 2, z: 4, core: 2. Of those that a mesh axis runs over, the one named last changes fastest.
Arguments:
- density: bfloat16 [4096, 4096], P('row', 'col'), as said below
- pattern: int32 [64, 64], P('row', 'col'), may hold values from 0 to 1, as said below
Outputs:
- updated: bfloat16 [4096, 4096], P('row', 'col')
- occupations: float32 [2], replicated
Inputs may be any that keep to these rules, and one draw needn't show every extreme that they name: pattern is symmetric, every diagonal block is 1. density is exactly symmetric and zero wherever pattern is 0.
All inputs are finite; a program needn't handle non-finite values.
Results may differ from a plain program's by a relative error of at most 0.0015.
Values may be sent and summed in bfloat16 or wider, within the bound.
A program may use at most 64 MiB of HBM per device.

v0:
```python
import jax
import jax.numpy as jnp
from jax import lax
from jax.sharding import PartitionSpec as P

BLK = 64


def expand_blocks(block_mask, width):
    block_rows, block_cols = block_mask.shape
    grid = jnp.broadcast_to(
        block_mask.astype(jnp.float32)[:, None, :, None], (block_rows, width, block_cols, width)
    )
    return grid.reshape(block_rows * width, block_cols * width)


def body(density, pattern):
    slab_rows, slab_cols = density.shape
    cell_mask = expand_blocks(pattern, BLK)
    column_panel = lax.all_gather(density, "row", axis=0, tiled=True)
    row_offset = lax.axis_index("row") * slab_rows
    col_offset = lax.axis_index("col") * slab_cols
    global_rows = row_offset + lax.iota(jnp.int32, slab_rows)
    global_cols = col_offset + lax.iota(jnp.int32, slab_cols)
    on_diagonal = global_rows[:, None] == global_cols[None, :]
    density_wide = density.astype(jnp.float32)
    trace_p_part = jnp.sum(jnp.where(on_diagonal, density_wide, 0.0))
    square = jnp.dot(
        lax.all_gather(density, "col", axis=1, tiled=True),
        column_panel,
        preferred_element_type=jnp.float32,
    )
    square = square * cell_mask
    trace_c_part = jnp.sum(jnp.where(on_diagonal, square, 0.0))
    trace_p, trace_c = lax.psum((trace_p_part, trace_c_part), ("row", "col"))
    order_total = slab_rows * lax.axis_size("row")
    take_square = trace_p > 1.0 * order_total
    updated = jnp.where(take_square, square, cell_mask * (2.0 * density_wide - square))
    trace_new = jnp.where(take_square, trace_c, 2.0 * trace_p - trace_c)
    occupations = jnp.stack([trace_p, trace_new]) / order_total
    return (updated.astype(jnp.bfloat16), occupations)


def solution(mesh):
    placed = (P("row", "col"), P("row", "col"))
    return jax.shard_map(
        body, mesh=mesh, in_specs=placed, out_specs=(P("row", "col"), P()), check_vma=False
    )
```

profile of v0, /device:TPU:0, one launch (start us, length us, event | category | flops | bytes accessed | tf_op | source)
XLA Modules:
  0.0 212.4 jit_solution(5599611315656936817)
XLA Ops:
  7.2 0.0 copy-start.1
  7.2 0.0 all-gather.3.cloned.1.call-start
  7.2 0.7 all-gather.3.cloned.1.call-update
  7.9 0.0 all-gather.5.cloned.1.call-start
  8.0 0.7 all-gather.5.cloned.1.call-update
  8.7 0.0 copy-done.1
  8.7 2.3 %broadcast_in_dim.14 = f32[8,64,16,64]{3,2,1,0:T(8,128)} broadcast(f32[8,16]{1,0:T(8,128)S(1)} %convert_element_type.10), dimensions={0,2} | broadcast | bytes 2097664 | tf_op jit(solution)/shard_map/broadcast_in_dim | solution.py:11
  11.0 0.0 copy-start
  11.0 3.6 %reshape.16 = f32[512,1024]{1,0:T(8,128)S(1)} reshape(f32[8,64,16,64]{3,2,1,0:T(8,128)} %broadcast_in_dim.14) | data formatting | bytes 4194304 | tf_op jit(solution)/shard_map/reshape | solution.py:14
  14.6 78.5 %all-gather.3.cloned.1.call-done = bf16[512,4096]{1,0:T(8,128)(2,1)} async-done(((bf16[512,1024]{1,0:T(8,128)(2,1)}), bf16[512,4096]{1,0:T(8,128)(2,1)}) %all-gather.3.cloned.1.call-update) | async-done | bytes 4194320 | tf_op jit(solution)/shard_map/all_gather | solution.py:29
  93.1 54.8 %all-gather.5.cloned.1.call-done = bf16[4096,1024]{1,0:T(8,128)(2,1)} async-done(((bf16[512,1024]{1,0:T(8,128)(2,1)}), bf16[4096,1024]{1,0:T(8,128)(2,1)}) %all-gather.5.cloned.1.call-update) | async-done | bytes 8388624 | tf_op jit(solution)/shard_map/all_gather | solution.py:20
  147.9 0.0 copy-done
  147.9 11.1 %fusion.5 = (f32[]{:T(128)}, f32[]{:T(128)}, f32[512,1024]{1,0:T(8,128)}) fusion(f32[512,1024]{1,0:T(8,128)S(1)} %reshape.16, s32[1024]{0:T(1024)S(1)} %iota_add_fusion, s32[512]{0:T(512)S(1)} %iota_add_fusion.1, bf16[512,1024]{1,0:T(8,128)(2,1)S(1)} %copy-done, bf16[512,4096]{1,0:T(8,128)(2,1)} %all-gather.3.cloned.1.call-done, ...), kind=kOutput, calls=%fused_computation.8 | convolution fusion | flops 4298637312 | bytes 17831944 | tf_op jit(solution)/shard_map/dot_general | solution.py:28
  159.0 39.6 %all-reduce = (f32[]{:T(128)}, f32[]{:T(128)}) all-reduce(f32[]{:T(128)} %get-tuple-element.3, f32[]{:T(128)} %get-tuple-element.2), channel_id=1, replica_groups=mesh['row'=8,'col'=4] {'row','col'}, use_global_device_ids=true, to_apply=%region_1.2 | all-reduce | flops 2 | bytes 16 | tf_op jit(solution)/shard_map/psum | solution.py:35
  201.2 3.2 %fusion.3 = bf16[512,1024]{1,0:T(8,128)(2,1)} fusion(f32[512,1024]{1,0:T(8,128)S(1)} %reshape.16, bf16[512,1024]{1,0:T(8,128)(2,1)S(1)} %copy-done, f32[512,1024]{1,0:T(8,128)} %get-tuple-element.6, pred[]{:T(512)S(6)} %gt.3), kind=kLoop, calls=%fused_computation.6 | loop fusion | flops 3670016 | bytes 6291457 | tf_op jit(solution)/shard_map/convert_element_type | solution.py:41
  204.3 1.2 maximum_multiply_fusion
  (3 shorter events, 0.0 us)
Async XLA Ops:
  7.2 1.5 copy-start.1
  7.2 85.9 %all-gather.3.cloned.1.call-start = ((), (), s32[]{:S(2)}) async-start(), calls=%async_computation | async-start | bytes 5242880 | tf_op jit(solution)/shard_map/all_gather | solution.py:29
  7.9 140.0 %all-gather.5.cloned.1.call-start = ((), (), s32[]{:S(2)}) async-start(), calls=%async_computation.1 | async-start | bytes 9437184 | tf_op jit(solution)/shard_map/all_gather | solution.py:20
  11.0 136.9 %copy-start = (bf16[512,1024]{1,0:T(8,128)(2,1)S(1)}, bf16[512,1024]{1,0:T(8,128)(2,1)}, u32[]{:S(2)}) copy-start(bf16[512,1024]{1,0:T(8,128)(2,1)} %param.2) | copy-start | bytes 3145732
Sparse Core Ops, SparseCore 0:
  9.6 83.4 all-gather.2
  95.0 52.9 all-gather.4
where the time goes:
time: 213 us; the launch traced here: 212 us
  waiting for transfers between devices  135 us (63%)
  blocking collectives  39.6 us (19%)
  between operations  16.7 us (8%)
  matrix products  11.1 us (5%)
  local copies, waits for them, and re-layouts  5.88 us (3%)
  other arithmetic  4.4 us (2%)
    all_gather x1, waiting for transfers between devices, body(): lax.all_gather(density, 'col', axis=1, tiled=True)  78.5 us
    all_gather x1, waiting for transfers between devices, body(): column_panel = lax.all_gather(density, 'row', axis=0, tiled=True)  54.8 us
    psum x1, blocking collectives, body(): trace_p, trace_c = lax.psum((trace_p_part, trace_c_part), ('row', 'col'))  39.6 us
    dot_general x1, matrix products, body(): jnp.dot(lax.all_gather(density, 'col', axis=1, tiled=True), column_panel,...  11.1 us
  transfers between devices with their start and end apart: 2, of which 2 were waited for; matrix products, arithmetic and copies ran while one was open for 3% of the time, Pallas kernels for 0%

commit v1 on v0

--- a/solution.py
+++ b/solution.py
@@ -4,6 +4,22 @@
 from jax.sharding import PartitionSpec as P
 
 BLK = 64
+
+
+def gather_around(x, axis, dim):
+    ways, here, step = (lax.axis_size(axis), lax.axis_index(axis), x.shape[dim])
+    shape = [n * ways if d == dim else n for d, n in enumerate(x.shape)]
+    full = lax.dynamic_update_slice_in_dim(jnp.zeros(shape, x.dtype), x, here * step, axis=dim)
+    going_up = going_down = x
+    for far in range(1, ways // 2 + 1):
+        going_up = lax.ppermute(going_up, axis, [(d, (d + 1) % ways) for d in range(ways)])
+        full = lax.dynamic_update_slice_in_dim(full, going_up, (here - far) % ways * step, axis=dim)
+        if 2 * far < ways:
+            going_down = lax.ppermute(going_down, axis, [(d, (d - 1) % ways) for d in range(ways)])
+            full = lax.dynamic_update_slice_in_dim(
+                full, going_down, (here + far) % ways * step, axis=dim
+            )
+    return full
 
 
 def expand_blocks(block_mask, width):
@@ -26,9 +42,7 @@
     density_wide = density.astype(jnp.float32)
     trace_p_part = jnp.sum(jnp.where(on_diagonal, density_wide, 0.0))
     square = jnp.dot(
-        lax.all_gather(density, "col", axis=1, tiled=True),
-        column_panel,
-        preferred_element_type=jnp.float32,
+        gather_around(density, "col", 1), column_panel, preferred_element_type=jnp.float32
     )
     square = square * cell_mask
     trace_c_part = jnp.sum(jnp.where(on_diagonal, square, 0.0))

time: 213 us -> 148 us (0.69)
  waiting for transfers between devices: 135 us -> 53.7 us
  local copies, waits for them, and re-layouts: 5.88 us -> 17 us
  starting transfers between devices: 0.08 us -> 5.21 us
    all_gather x1 -> x0, waiting for transfers between devices: 78.5 us -> none  [body(): lax.all_gather(density, 'col', axis=1, tiled=True)]
    all_gather x1, waiting for transfers between devices: 54.8 us -> 0.01 us  [body(): column_panel = lax.all_gather(density, 'row', axis=0, tiled=True)]
    ppermute x0 -> x3, waiting for transfers between devices: none -> 53 us  [the longest x2 44.9 us: gather_around(): lax.ppermute(going_up, axis, [(d, (d + 1) % ways) for d in range(ways)])]
    dynamic_update_slice x0 -> x4, local copies, waits for them, and re-layouts: none -> 8.11 us  [the longest x2 4.68 us: gather_around(): lax.dynamic_update_slice_in_dim(full, going_up, (here - far) % ways * ste...]
    ppermute x0 -> x3, starting transfers between devices: none -> 5.17 us  [the longest x2 3.08 us: gather_around(): lax.ppermute(going_up, axis, [(d, (d + 1) % ways) for d in range(ways)])]
    broadcast_in_dim x0 -> x1, local copies, waits for them, and re-layouts: none -> 2.48 us  [gather_around(): jnp.zeros(shape, x.dtype)]
  transfers between devices with their start and end apart: 2 -> 4, of which waited for: 2 -> 3; matrix products, arithmetic and copies ran while one was open for 3% -> 12% of each run, Pallas kernels for 0% -> 0%
where the time goes in v1:
time: 148 us; the launch traced here: 147 us
  waiting for transfers between devices  53.7 us (36%)
  blocking collectives  38.8 us (26%)
  local copies, waits for them, and re-layouts  17 us (11%)
  between operations  16.5 us (11%)
  matrix products  11.1 us (8%)
  starting transfers between devices  5.21 us (4%)
  other arithmetic  5.01 us (3%)
    ppermute x2, waiting for transfers between devices, gather_around(): lax.ppermute(going_up, axis, [(d, (d + 1) % ways) for d in range(ways)])  44.9 us
    psum x1, blocking collectives, body(): trace_p, trace_c = lax.psum((trace_p_part, trace_c_part), ('row', 'col'))  38.8 us
    dot_general x1, matrix products, body(): jnp.dot(gather_around(density, 'col', 1), column_panel, preferred_element...  11.1 us
    ppermute x1, waiting for transfers between devices, gather_around(): lax.ppermute(going_down, axis, [(d, (d - 1) % ways) for d in range(ways)])  8.13 us
    dynamic_update_slice x2, local copies, waits for them, and re-layouts, gather_around(): lax.dynamic_update_slice_in_dim(full, going_up, (here - far) % ways * ste...  4.68 us
    reshape x1, local copies, waits for them, and re-layouts, expand_blocks(): return grid.reshape(block_rows * width, block_cols * width)  4.1 us
    convert_element_type x1, other arithmetic, body(): return (updated.astype(jnp.bfloat16), occupations)  3.17 us
    ppermute x2, starting transfers between devices, gather_around(): lax.ppermute(going_up, axis, [(d, (d + 1) % ways) for d in range(ways)])  3.08 us
  transfers between devices with their start and end apart: 4, of which 3 were waited for; matrix products, arithmetic and copies ran while one was open for 12% of the time, Pallas kernels for 0%

profile of v1, /device:TPU:0, one launch (start us, length us, event | category | flops | bytes accessed | tf_op | source)
XLA Modules:
  0.0 147.3 jit_solution(14228139046654437082)
XLA Ops:
  7.2 0.0 all-gather.2.cloned.1.call-start
  7.2 0.7 all-gather.2.cloned.1.call-update
  7.9 3.1 %collective-permute-start = (bf16[512,1024]{1,0:T(8,128)(2,1)}, bf16[512,1024]{1,0:T(8,128)(2,1)}, u32[]{:S(2)}, u32[]{:S(2)}) collective-permute-start(bf16[512,1024]{1,0:T(8,128)(2,1)} %param.2), channel_id=1, source_target_pairs={{0,1},{1,2},{2,3},{3,0},{4,5},{5,6},{6,7},{7,4},{8,9},{9,10},{10,1... | collective-permute-start | bytes 3145736 | tf_op jit(solution)/shard_map/ppermute | solution.py:15
  11.0 2.1 %collective-permute-start.1 = (bf16[512,1024]{1,0:T(8,128)(2,1)}, bf16[512,1024]{1,0:T(8,128)(2,1)}, u32[]{:S(2)}, u32[]{:S(2)}) collective-permute-start(bf16[512,1024]{1,0:T(8,128)(2,1)} %param.2), channel_id=1, source_target_pairs={{0,3},{1,0},{2,1},{3,2},{4,7},{5,4},{6,5},{7,6},{8,11},{9,8},{10,9... | collective-permute-start | bytes 3145736 | tf_op jit(solution)/shard_map/ppermute | solution.py:18
  13.1 24.3 %collective-permute-done = bf16[512,1024]{1,0:T(8,128)(2,1)} collective-permute-done((bf16[512,1024]{1,0:T(8,128)(2,1)}, bf16[512,1024]{1,0:T(8,128)(2,1)}, u32[]{:S(2)}, u32[]{:S(2)}) %collective-permute-start) | collective-permute-done | bytes 1048608 | tf_op jit(solution)/shard_map/ppermute | solution.py:15
  37.4 0.0 collective-permute-start.2
  37.4 0.7 convert_element_type.10
  38.0 2.3 %broadcast_in_dim.18 = f32[8,64,16,64]{3,2,1,0:T(8,128)} broadcast(f32[8,16]{1,0:T(8,128)S(1)} %convert_element_type.10), dimensions={0,2} | broadcast | bytes 2097664 | tf_op jit(solution)/shard_map/broadcast_in_dim | solution.py:27
  40.4 0.0 copy-start
  40.4 4.1 %reshape.16 = f32[512,1024]{1,0:T(8,128)S(1)} reshape(f32[8,64,16,64]{3,2,1,0:T(8,128)} %broadcast_in_dim.18) | data formatting | bytes 4194304 | tf_op jit(solution)/shard_map/reshape | solution.py:30
  44.5 2.5 %broadcast_in_dim.17 = bf16[512,4096]{1,0:T(8,128)(2,1)} broadcast(bf16[]{:T(256)} %constant.46.clone.1), dimensions={} | broadcast | bytes 4194306 | tf_op jit(solution)/shard_map/broadcast_in_dim | solution.py:12
  47.0 0.0 copy-done
  47.0 1.1 constant_dynamic-update-slice_fusion.3
  48.1 2.3 %constant_dynamic-update-slice_fusion.2 = bf16[512,4096]{1,0:T(8,128)(2,1)} fusion(bf16[512,4096]{1,0:T(8,128)(2,1)} %constant_dynamic-update-slice_fusion.3, bf16[512,1024]{1,0:T(8,128)(2,1)} %collective-permute-done, s32[]{:T(128)S(6)} %select_n.50), kind=kLoop, calls=%fused_computation.13 | loop fusion | bytes 2097156 | tf_op jit(solution)/shard_map/dynamic_update_slice | solution.py:16
  50.5 8.1 %collective-permute-done.1 = bf16[512,1024]{1,0:T(8,128)(2,1)} collective-permute-done((bf16[512,1024]{1,0:T(8,128)(2,1)}, bf16[512,1024]{1,0:T(8,128)(2,1)}, u32[]{:S(2)}, u32[]{:S(2)}) %collective-permute-start.1) | collective-permute-done | bytes 1048608 | tf_op jit(solution)/shard_map/ppermute | solution.py:18
  58.6 2.3 %constant_dynamic-update-slice_fusion.1 = bf16[512,4096]{1,0:T(8,128)(2,1)} fusion(bf16[512,4096]{1,0:T(8,128)(2,1)} %constant_dynamic-update-slice_fusion.2, bf16[512,1024]{1,0:T(8,128)(2,1)} %collective-permute-done.1, s32[]{:T(128)S(6)} %select_n.52), kind=kLoop, calls=%fused_computation.12 | loop fusion | bytes 2097156 | tf_op jit(solution)/shard_map/dynamic_update_slice | solution.py:19
  60.9 20.6 %collective-permute-done.2 = bf16[512,1024]{1,0:T(8,128)(2,1)} collective-permute-done((bf16[512,1024]{1,0:T(8,128)(2,1)}, bf16[512,1024]{1,0:T(8,128)(2,1)}, u32[]{:S(2)}, u32[]{:S(2)}) %collective-permute-start.2) | collective-permute-done | bytes 1048608 | tf_op jit(solution)/shard_map/ppermute | solution.py:15
  81.5 2.4 %constant_dynamic-update-slice_fusion = bf16[512,4096]{1,0:T(8,128)(2,1)} fusion(bf16[512,4096]{1,0:T(8,128)(2,1)} %constant_dynamic-update-slice_fusion.1, bf16[512,1024]{1,0:T(8,128)(2,1)} %collective-permute-done.2, s32[]{:T(128)S(6)} %select_n.54), kind=kLoop, calls=%fused_computation.11 | loop fusion | bytes 2097156 | tf_op jit(solution)/shard_map/dynamic_update_slice | solution.py:16
  83.8 0.0 all-gather.2.cloned.1.call-done
  83.8 11.1 %fusion.5 = (f32[]{:T(128)}, f32[]{:T(128)}, f32[512,1024]{1,0:T(8,128)}) fusion(f32[512,1024]{1,0:T(8,128)S(1)} %reshape.16, s32[1024]{0:T(1024)S(1)} %iota_add_fusion, s32[512]{0:T(512)S(1)} %iota_add_fusion.1, bf16[512,1024]{1,0:T(8,128)(2,1)S(1)} %copy-done, bf16[512,4096]{1,0:T(8,128)(2,1)} %constant_dynamic-update-slice_fusion, ...), kind=kOutput, calls=%fused_computation.8 | convolution fusion | flops 4298637312 | bytes 17831944 | tf_op jit(solution)/shard_map/dot_general | solution.py:44
  94.9 38.8 %all-reduce = (f32[]{:T(128)}, f32[]{:T(128)}) all-reduce(f32[]{:T(128)} %get-tuple-element.3, f32[]{:T(128)} %get-tuple-element.2), channel_id=1, replica_groups=mesh['row'=8,'col'=4] {'row','col'}, use_global_device_ids=true, to_apply=%region_1.2 | all-reduce | flops 2 | bytes 16 | tf_op jit(solution)/shard_map/psum | solution.py:49
  136.2 3.2 %fusion.3 = bf16[512,1024]{1,0:T(8,128)(2,1)} fusion(f32[512,1024]{1,0:T(8,128)S(1)} %reshape.16, bf16[512,1024]{1,0:T(8,128)(2,1)S(1)} %copy-done, f32[512,1024]{1,0:T(8,128)} %get-tuple-element.6, pred[]{:T(512)S(6)} %gt.3), kind=kLoop, calls=%fused_computation.6 | loop fusion | flops 3670016 | bytes 6291457 | tf_op jit(solution)/shard_map/convert_element_type | solution.py:55
  139.3 1.1 maximum_multiply_fusion
  (2 shorter events, 0.0 us)
Async XLA Ops:
  7.2 76.7 %all-gather.2.cloned.1.call-start = ((), (), s32[]{:S(2)}) async-start(), calls=%async_computation | async-start | bytes 9437184 | tf_op jit(solution)/shard_map/all_gather | solution.py:36
  7.9 29.5 %collective-permute-start = (bf16[512,1024]{1,0:T(8,128)(2,1)}, bf16[512,1024]{1,0:T(8,128)(2,1)}, u32[]{:S(2)}, u32[]{:S(2)}) collective-permute-start(bf16[512,1024]{1,0:T(8,128)(2,1)} %param.2), channel_id=1, source_target_pairs={{0,1},{1,2},{2,3},{3,0},{4,5},{5,6},{6,7},{7,4},{8,9},{9,10},{10,1... | collective-permute-start | bytes 3145736 | tf_op jit(solution)/shard_map/ppermute | solution.py:15
  11.0 47.6 %collective-permute-start.1 = (bf16[512,1024]{1,0:T(8,128)(2,1)}, bf16[512,1024]{1,0:T(8,128)(2,1)}, u32[]{:S(2)}, u32[]{:S(2)}) collective-permute-start(bf16[512,1024]{1,0:T(8,128)(2,1)} %param.2), channel_id=1, source_target_pairs={{0,3},{1,0},{2,1},{3,2},{4,7},{5,4},{6,5},{7,6},{8,11},{9,8},{10,9... | collective-permute-start | bytes 3145736 | tf_op jit(solution)/shard_map/ppermute | solution.py:18
  37.4 44.1 %collective-permute-start.2 = (bf16[512,1024]{1,0:T(8,128)(2,1)}, bf16[512,1024]{1,0:T(8,128)(2,1)}, u32[]{:S(2)}, u32[]{:S(2)}) collective-permute-start(bf16[512,1024]{1,0:T(8,128)(2,1)} %collective-permute-done), channel_id=1, source_target_pairs={{0,1},{1,2},{2,3},{3,0},{4,5},{5,6},{6,7},{7,4},{8,9},{9,10},{10,1... | collective-permute-start | bytes 3145736 | tf_op jit(solution)/shard_map/ppermute | solution.py:15
  40.4 6.6 %copy-start = (bf16[512,1024]{1,0:T(8,128)(2,1)S(1)}, bf16[512,1024]{1,0:T(8,128)(2,1)}, u32[]{:S(2)}) copy-start(bf16[512,1024]{1,0:T(8,128)(2,1)} %param.2) | copy-start | bytes 3145732
Sparse Core Ops, SparseCore 0:
  9.9 57.0 all-gather.1

commit v2 on v0

--- a/solution.py
+++ b/solution.py
@@ -4,6 +4,7 @@
 from jax.sharding import PartitionSpec as P
 
 BLK = 64
+remake_sums_all = lambda xs: jax.lax.psum(jax.lax.psum(xs, "col"), "row")
 
 
 def expand_blocks(block_mask, width):
@@ -32,7 +33,7 @@
     )
     square = square * cell_mask
     trace_c_part = jnp.sum(jnp.where(on_diagonal, square, 0.0))
-    trace_p, trace_c = lax.psum((trace_p_part, trace_c_part), ("row", "col"))
+    trace_p, trace_c = remake_sums_all((trace_p_part, trace_c_part))
     order_total = slab_rows * lax.axis_size("row")
     take_square = trace_p > 1.0 * order_total
     updated = jnp.where(take_square, square, cell_mask * (2.0 * density_wide - square))

time: 213 us -> 198 us (0.930)
  blocking collectives: 39.6 us -> 24.8 us
    psum x1 -> x2, blocking collectives: 39.6 us -> 24.8 us  [remake_sums_all = lambda xs: jax.lax.psum(jax.lax.psum(xs, 'col'), 'row')]
where the time goes in v2:
time: 198 us
  waiting for transfers between devices  135 us (68%)
  blocking collectives  24.8 us (13%)
  between operations  16.8 us (8%)
  matrix products  11.1 us (6%)
  local copies, waits for them, and re-layouts  5.89 us (3%)
  other arithmetic  4.45 us (2%)
    all_gather x1, waiting for transfers between devices, body(): lax.all_gather(density, 'col', axis=1, tiled=True)  78.5 us
    all_gather x1, waiting for transfers between devices, body(): column_panel = lax.all_gather(density, 'row', axis=0, tiled=True)  54.8 us
    psum x2, blocking collectives, remake_sums_all = lambda xs: jax.lax.psum(jax.lax.psum(xs, 'col'), 'row')  24.8 us
    dot_general x1, matrix products, body(): jnp.dot(lax.all_gather(density, 'col', axis=1, tiled=True), column_panel,...  11.1 us
  transfers between devices with their start and end apart: 2, of which 2 were waited for; matrix products, arithmetic and copies ran while one was open for 3% of the time, Pallas kernels for 0%

profile of v2, /device:TPU:0, one launch (start us, length us, event | category | flops | bytes accessed | tf_op | source)
XLA Modules:
  0.0 197.8 jit_solution(15971748451290700694)
XLA Ops:
  7.2 0.0 copy-start.1
  7.2 0.0 all-gather.3.cloned.1.call-start
  7.2 0.7 all-gather.3.cloned.1.call-update
  7.9 0.0 all-gather.5.cloned.1.call-start
  8.0 0.7 all-gather.5.cloned.1.call-update
  8.7 0.0 copy-done.1
  8.7 2.3 %broadcast_in_dim.14 = f32[8,64,16,64]{3,2,1,0:T(8,128)} broadcast(f32[8,16]{1,0:T(8,128)S(1)} %convert_element_type.10), dimensions={0,2} | broadcast | bytes 2097664 | tf_op jit(solution)/shard_map/broadcast_in_dim | solution.py:12
  11.0 0.0 copy-start
  11.0 3.6 %reshape.16 = f32[512,1024]{1,0:T(8,128)S(1)} reshape(f32[8,64,16,64]{3,2,1,0:T(8,128)} %broadcast_in_dim.14) | data formatting | bytes 4194304 | tf_op jit(solution)/shard_map/reshape | solution.py:15
  14.6 78.5 %all-gather.3.cloned.1.call-done = bf16[512,4096]{1,0:T(8,128)(2,1)} async-done(((bf16[512,1024]{1,0:T(8,128)(2,1)}), bf16[512,4096]{1,0:T(8,128)(2,1)}) %all-gather.3.cloned.1.call-update) | async-done | bytes 4194320 | tf_op jit(solution)/shard_map/all_gather | solution.py:30
  93.1 54.8 %all-gather.5.cloned.1.call-done = bf16[4096,1024]{1,0:T(8,128)(2,1)} async-done(((bf16[512,1024]{1,0:T(8,128)(2,1)}), bf16[4096,1024]{1,0:T(8,128)(2,1)}) %all-gather.5.cloned.1.call-update) | async-done | bytes 8388624 | tf_op jit(solution)/shard_map/all_gather | solution.py:21
  147.9 0.0 copy-done
  147.9 11.1 %fusion.5 = (f32[]{:T(128)}, f32[]{:T(128)}, f32[512,1024]{1,0:T(8,128)}) fusion(f32[512,1024]{1,0:T(8,128)S(1)} %reshape.16, s32[1024]{0:T(1024)S(1)} %iota_add_fusion, s32[512]{0:T(512)S(1)} %iota_add_fusion.1, bf16[512,1024]{1,0:T(8,128)(2,1)S(1)} %copy-done, bf16[512,4096]{1,0:T(8,128)(2,1)} %all-gather.3.cloned.1.call-done, ...), kind=kOutput, calls=%fused_computation.8 | convolution fusion | flops 4298637312 | bytes 17831944 | tf_op jit(solution)/shard_map/dot_general | solution.py:29
  159.0 12.3 %all-reduce.1 = (f32[]{:T(128)}, f32[]{:T(128)}) all-reduce(f32[]{:T(128)} %get-tuple-element.3, f32[]{:T(128)} %get-tuple-element.2), channel_id=1, replica_groups=mesh['row'=8,'col'=4] {'col'}, use_global_device_ids=true, to_apply=%region_1.2 | all-reduce | flops 2 | bytes 16 | tf_op jit(solution)/shard_map/psum | solution.py:7
  171.3 12.5 %all-reduce = (f32[]{:T(128)}, f32[]{:T(128)}) all-reduce(f32[]{:T(128)} %get-tuple-element.6, f32[]{:T(128)} %get-tuple-element.7), channel_id=1, replica_groups=mesh['row'=8,'col'=4] {'row'}, use_global_device_ids=true, to_apply=%region_2.3 | all-reduce | flops 2 | bytes 16 | tf_op jit(solution)/shard_map/psum | solution.py:7
  186.5 3.2 %fusion.3 = bf16[512,1024]{1,0:T(8,128)(2,1)} fusion(f32[512,1024]{1,0:T(8,128)S(1)} %reshape.16, bf16[512,1024]{1,0:T(8,128)(2,1)S(1)} %copy-done, f32[512,1024]{1,0:T(8,128)} %get-tuple-element.8, pred[]{:T(512)S(6)} %gt.3), kind=kLoop, calls=%fused_computation.6 | loop fusion | flops 3670016 | bytes 6291457 | tf_op jit(solution)/shard_map/convert_element_type | solution.py:42
  189.7 1.3 maximum_multiply_fusion
  (3 shorter events, 0.0 us)
Async XLA Ops:
  7.2 1.5 copy-start.1
  7.2 85.9 %all-gather.3.cloned.1.call-start = ((), (), s32[]{:S(2)}) async-start(), calls=%async_computation | async-start | bytes 5242880 | tf_op jit(solution)/shard_map/all_gather | solution.py:30
  7.9 140.0 %all-gather.5.cloned.1.call-start = ((), (), s32[]{:S(2)}) async-start(), calls=%async_computation.1 | async-start | bytes 9437184 | tf_op jit(solution)/shard_map/all_gather | solution.py:21
  11.0 136.9 %copy-start = (bf16[512,1024]{1,0:T(8,128)(2,1)S(1)}, bf16[512,1024]{1,0:T(8,128)(2,1)}, u32[]{:S(2)}) copy-start(bf16[512,1024]{1,0:T(8,128)(2,1)} %param.2) | copy-start | bytes 3145732
Sparse Core Ops, SparseCore 0:
  9.6 83.4 all-gather.2
  95.0 52.9 all-gather.4
